TPU v7x, 32 devices: a whole 2x2x4 slice. The times are simulated.
32 devices in a mesh: dp: 16 (over z, x, core), tensor: 2 (over y).
Axes of the slice: x: 2, y: 2, z: 4, core: 2. Of those that a mesh axis runs over, the one named last changes fastest.
Arguments:
- inputs: bfloat16 [12288, 768], P('dp'), may hold values from -6 to 6
- clip_ids: int32 [12288], replicated, may hold values from 0 to 11, never falling along the last dimension, each value on 1 to 1500 neighbouring positions
- attn_gain: bfloat16 [768], replicated, may hold values from 0.5 to 1.5
- attn_shift: bfloat16 [768], replicated, may hold values from -1.75 to 1.75
- w_query: bfloat16 [768, 768], P(None, 'tensor'), may hold values from -0.21875 to 0.21875
- query_bias: bfloat16 [768], P('tensor'), may hold values from -1.75 to 1.75
- w_key: bfloat16 [768, 768], P(None, 'tensor'), may hold values from -0.21875 to 0.21875
- w_value: bfloat16 [768, 768], P(None, 'tensor'), may hold values from -0.21875 to 0.21875
- value_bias: bfloat16 [768], P('tensor'), may hold values from -3 to 3
- w_out: bfloat16 [768, 768], P('tensor'), may hold values from -4 to 4
- out_bias: bfloat16 [768], replicated, may hold values from -1.75 to 1.75
- mlp_gain: bfloat16 [768], replicated, may hold values from 0.5 to 1.5
- mlp_shift: bfloat16 [768], replicated, may hold values from -1.75 to 1.75
- w_fc1: bfloat16 [768, 3072], P(None, 'tensor'), may hold values from -0.21875 to 0.21875
- fc1_bias: bfloat16 [3072], P('tensor'), may hold values from -3 to 3
- w_fc2: bfloat16 [3072, 768], P('tensor'), may hold values from -0.109375 to 0.109375
- fc2_bias: bfloat16 [768], replicated, may hold values from -1.75 to 1.75
- cotangent: bfloat16 [12288, 768], P('dp'), may hold values from -6 to 6
Outputs:
- layer_out: bfloat16 [12288, 768], P('dp')
- inputs_grad: float32 [12288, 768], P('dp')
- attn_gain_grad: float32 [768], replicated
- attn_shift_grad: float32 [768], replicated
- w_query_grad: float32 [768, 768], P(None, 'tensor')
- query_bias_grad: float32 [768], P('tensor')
- w_key_grad: float32 [768, 768], P(None, 'tensor')
- w_value_grad: float32 [768, 768], P(None, 'tensor')
- value_bias_grad: float32 [768], P('tensor')
- w_out_grad: float32 [768, 768], P('tensor')
- out_bias_grad: float32 [768], replicated
- mlp_gain_grad: float32 [768], replicated
- mlp_shift_grad: float32 [768], replicated
- w_fc1_grad: float32 [768, 3072], P(None, 'tensor')
- fc1_bias_grad: float32 [3072], P('tensor')
- w_fc2_grad: float32 [3072, 768], P('tensor')
- fc2_bias_grad: float32 [768], replicated
Inputs may be any that keep to these rules, and one draw needn't show every extreme that they name: `clip_ids`: clip numbers never fall along the tokens; each of the 12 clips holds 1 to 1500 consecutive tokens, and one holds exactly 1500.
All inputs are finite; a program needn't handle non-finite values.
Results may differ from a plain program's by a relative error of at most 0.012.
Values may be sent and summed in bfloat16 or wider, within the bound.
A program may use at most 128 MiB of HBM per device.

v0:
```python
import jax
import jax.numpy as jnp
from jax import lax
from jax.sharding import PartitionSpec as P

HEAD_DIM = 64
REACH = 2


def from_behind(block, axis, distance):
    devices = range(lax.axis_size(axis))
    route = [(i - distance, i) for i in devices if i - distance in devices]
    return lax.ppermute(block, axis, route)


def layer_norm(values, gain_row, bias_row):
    middle = jnp.mean(values, axis=-1, keepdims=True)
    centred = values - middle
    spread = jnp.mean(centred * centred, axis=-1, keepdims=True)
    return centred * lax.rsqrt(spread + 1e-05) * gain_row + bias_row


def exact_gelu(values):
    return jax.nn.gelu(values, approximate=False)


def matmul(left, right):
    return jnp.dot(left, right, preferred_element_type=jnp.float32)


def contract_rows(left, right):
    return lax.dot_general(
        left, right, (((0,), (0,)), ((), ())), preferred_element_type=jnp.float32
    )


def contract_cols(left, right):
    return lax.dot_general(
        left, right, (((1,), (1,)), ((), ())), preferred_element_type=jnp.float32
    )


def split_heads(values):
    return values.reshape(values.shape[0], values.shape[1] // HEAD_DIM, HEAD_DIM).transpose(1, 0, 2)


def join_heads(stacked):
    return stacked.transpose(1, 0, 2).reshape(stacked.shape[1], stacked.shape[0] * stacked.shape[2])


def on_device(
    inputs,
    clip_ids,
    attn_gain,
    attn_shift,
    w_query,
    query_bias,
    w_key,
    w_value,
    value_bias,
    w_out,
    out_bias,
    mlp_gain,
    mlp_shift,
    w_fc1,
    fc1_bias,
    w_fc2,
    fc2_bias,
    cotangent,
):
    height = inputs.shape[0]
    devices = lax.axis_size("dp")
    myself = lax.axis_index("dp")
    factor = HEAD_DIM ** (-0.5)
    offsets = list(range(-REACH, REACH + 1))

    def clip_block(offset):
        holder = myself + offset
        begin_at = jnp.clip(holder, 0, devices - 1) * height
        labels = lax.dynamic_slice_in_dim(clip_ids, begin_at, height)
        inside = jnp.logical_and(holder >= 0, holder < devices)
        return jnp.where(inside, labels, -1)

    own_labels = clip_block(0)
    key_labels = jnp.concatenate([clip_block(offset) for offset in offsets])
    allowed = own_labels[:, None] == key_labels[None, :]
    source = inputs.astype(jnp.float32)
    normed_one, norm_one_back = jax.vjp(
        layer_norm, source, attn_gain.astype(jnp.float32), attn_shift.astype(jnp.float32)
    )
    attn_input = normed_one.astype(jnp.bfloat16)
    queries = (matmul(attn_input, w_query) + query_bias.astype(jnp.float32)).astype(jnp.bfloat16)
    keys_own = matmul(attn_input, w_key).astype(jnp.bfloat16)
    values_own = (matmul(attn_input, w_value) + value_bias.astype(jnp.float32)).astype(jnp.bfloat16)
    key_parts = []
    value_parts = []
    for offset in offsets:
        if offset == 0:
            key_parts.append(keys_own)
            value_parts.append(values_own)
        else:
            moved_keys, moved_values = from_behind((keys_own, values_own), "dp", -offset)
            key_parts.append(moved_keys)
            value_parts.append(moved_values)
    query_heads = split_heads(queries)
    key_heads = split_heads(jnp.concatenate(key_parts))
    value_heads = split_heads(jnp.concatenate(value_parts))

    def attend(operands):
        query_one, key_one, value_one = operands
        scores = jnp.where(allowed, contract_cols(query_one, key_one) * factor, -1e30)
        largest = jnp.max(scores, axis=1, keepdims=True)
        expset = jnp.exp(scores - largest)
        totals = jnp.sum(expset, axis=1, keepdims=True)
        weights = (expset / totals).astype(jnp.bfloat16)
        mixed_one = matmul(weights, value_one)
        return (mixed_one.astype(jnp.bfloat16), largest[:, 0] + jnp.log(totals[:, 0]))

    head_out, log_totals = lax.map(attend, (query_heads, key_heads, value_heads))
    attn_mixed = join_heads(head_out)
    attn_total = lax.psum(matmul(attn_mixed, w_out), "tensor") + out_bias.astype(jnp.float32)
    residual = source + attn_total
    normed_two, norm_two_back = jax.vjp(
        layer_norm, residual, mlp_gain.astype(jnp.float32), mlp_shift.astype(jnp.float32)
    )
    mlp_input = normed_two.astype(jnp.bfloat16)
    preact = matmul(mlp_input, w_fc1) + fc1_bias.astype(jnp.float32)
    activated_full, gelu_back = jax.vjp(exact_gelu, preact)
    activated = activated_full.astype(jnp.bfloat16)
    mlp_total = lax.psum(matmul(activated, w_fc2).astype(jnp.bfloat16), "tensor").astype(
        jnp.float32
    ) + fc2_bias.astype(jnp.float32)
    layer_out = (residual + mlp_total).astype(jnp.bfloat16)
    out_grad_full = cotangent.astype(jnp.float32)
    fc2_bias_grad = jnp.sum(out_grad_full, axis=0)
    w_fc2_grad = contract_rows(activated, cotangent)
    (pre_full,) = gelu_back(contract_cols(cotangent, w_fc2))
    pre_grad = pre_full.astype(jnp.bfloat16)
    fc1_bias_grad = jnp.sum(pre_grad.astype(jnp.float32), axis=0)
    w_fc1_grad = contract_rows(mlp_input, pre_grad)
    mlp_in_grad = lax.psum(contract_cols(pre_grad, w_fc1), "tensor")
    resid_back, mlp_gain_grad, mlp_shift_grad = norm_two_back(mlp_in_grad)
    residual_grad = out_grad_full + resid_back
    attn_grad_low = residual_grad.astype(jnp.bfloat16)
    out_bias_grad = jnp.sum(attn_grad_low.astype(jnp.float32), axis=0)
    w_out_grad = contract_rows(attn_mixed, attn_grad_low)
    mixed_heads = split_heads(contract_cols(attn_grad_low, w_out).astype(jnp.bfloat16))

    def attend_back(operands):
        query_one, key_one, value_one, log_total, mixed_one = operands
        scores = jnp.where(allowed, contract_cols(query_one, key_one) * factor, -1e30)
        probs = jnp.exp(scores - log_total[:, None])
        probs_low = probs.astype(jnp.bfloat16)
        prob_grad = contract_cols(mixed_one, value_one)
        centre = jnp.sum(probs * prob_grad, axis=1, keepdims=True)
        score_grad = (probs * (prob_grad - centre)).astype(jnp.bfloat16)
        query_part = (matmul(score_grad, key_one) * factor).astype(jnp.bfloat16)
        key_part = contract_rows(score_grad, query_one) * factor
        value_part = contract_rows(probs_low, mixed_one)
        return (query_part, key_part, value_part)

    query_parts, key_grads, value_grads = lax.map(
        attend_back, (query_heads, key_heads, value_heads, log_totals, mixed_heads)
    )
    query_low = join_heads(query_parts)
    key_window_grad = join_heads(key_grads)
    value_window_grad = join_heads(value_grads)
    centre_row = REACH * height
    key_sum = key_window_grad[centre_row : centre_row + height]
    value_sum = value_window_grad[centre_row : centre_row + height]
    for position, offset in enumerate(offsets):
        if offset != 0:
            begin_row = position * height
            back_keys, back_values = (
                from_behind(
                    key_window_grad[begin_row : begin_row + height].astype(jnp.bfloat16),
                    "dp",
                    offset,
                ).astype(jnp.float32),
                from_behind(
                    value_window_grad[begin_row : begin_row + height].astype(jnp.bfloat16),
                    "dp",
                    offset,
                ).astype(jnp.float32),
            )
            key_sum = key_sum + back_keys
            value_sum = value_sum + back_values
    key_low = key_sum.astype(jnp.bfloat16)
    value_low = value_sum.astype(jnp.bfloat16)
    query_bias_grad = jnp.sum(query_low.astype(jnp.float32), axis=0)
    value_bias_grad = jnp.sum(value_low.astype(jnp.float32), axis=0)
    w_query_grad = contract_rows(attn_input, query_low)
    w_key_grad = contract_rows(attn_input, key_low)
    w_value_grad = contract_rows(attn_input, value_low)
    attn_in_part = (
        contract_cols(query_low, w_query)
        + contract_cols(key_low, w_key)
        + contract_cols(value_low, w_value)
    )
    attn_in_grad = lax.psum(attn_in_part.astype(jnp.bfloat16), "tensor").astype(jnp.float32)
    source_back, attn_gain_grad, attn_shift_grad = norm_one_back(attn_in_grad)
    inputs_grad = residual_grad + source_back
    (
        w_query_grad,
        query_bias_grad,
        w_key_grad,
        w_value_grad,
        value_bias_grad,
        w_out_grad,
        out_bias_grad,
        attn_gain_grad,
        attn_shift_grad,
        w_fc1_grad,
        fc1_bias_grad,
        w_fc2_grad,
        fc2_bias_grad,
        mlp_gain_grad,
        mlp_shift_grad,
    ) = lax.psum(
        (
            w_query_grad,
            query_bias_grad,
            w_key_grad,
            w_value_grad,
            value_bias_grad,
            w_out_grad,
            out_bias_grad,
            attn_gain_grad,
            attn_shift_grad,
            w_fc1_grad,
            fc1_bias_grad,
            w_fc2_grad,
            fc2_bias_grad,
            mlp_gain_grad,
            mlp_shift_grad,
        ),
        "dp",
    )
    return (
        layer_out,
        inputs_grad,
        attn_gain_grad,
        attn_shift_grad,
        w_query_grad,
        query_bias_grad,
        w_key_grad,
        w_value_grad,
        value_bias_grad,
        w_out_grad,
        out_bias_grad,
        mlp_gain_grad,
        mlp_shift_grad,
        w_fc1_grad,
        fc1_bias_grad,
        w_fc2_grad,
        fc2_bias_grad,
    )


def solution(mesh):
    in_specs = (
        P("dp", None),
        P(),
        P(),
        P(),
        P(None, "tensor"),
        P("tensor"),
        P(None, "tensor"),
        P(None, "tensor"),
        P("tensor"),
        P("tensor", None),
        P(),
        P(),
        P(),
        P(None, "tensor"),
        P("tensor"),
        P("tensor", None),
        P(),
        P("dp", None),
    )
    out_specs = (
        P("dp", None),
        P("dp", None),
        P(),
        P(),
        P(None, "tensor"),
        P("tensor"),
        P(None, "tensor"),
        P(None, "tensor"),
        P("tensor"),
        P("tensor", None),
        P(),
        P(),
        P(),
        P(None, "tensor"),
        P("tensor"),
        P("tensor", None),
        P(),
    )
    return jax.shard_map(
        on_device, mesh=mesh, in_specs=in_specs, out_specs=out_specs, check_vma=False
    )
```

profile of v0, /device:TPU:0, one launch (start us, length us, event | category | flops | bytes accessed | tf_op | source)
XLA Modules:
  0.0 940.8 jit_solution(11370151416153895606)
XLA Ops:
  15.0 5.8 collective-permute-start
  27.3 6.1 collective-permute-start.4
  44.1 8.9 collective-permute-done
  67.8 4.5 copy.40
  72.3 6.5 copy.42
  90.4 4.5 copy.41
  94.9 6.5 copy.43
  102.2 65.1 %while.28 = (s32[]{:T(128)}, bf16[6,768,64]{1,2,0:T(8,128)(2,1)}, f32[6,768]{1,0:T(8,128)}, bf16[6,768,64]{2,1,0:T(8,128)(2,1)}, bf16[6,3840,64]{2,1,0:T(8,128)(...) while((s32[]{:T(128)}, bf16[6,768,64]{1,2,0:T(8,128)(2,1)}, ...), condition=%wide.region_5.6_spmd.clone, body=%wide.region_2.5_spmd.clone.sunk | while | flops 781565184 | bytes 37708912 | solution.py:119
  107.3 4.4 fusion.155
  118.2 4.4 fusion.155
  129.0 4.4 fusion.155
  139.8 4.4 fusion.155
  150.7 4.4 fusion.155
  161.5 4.4 fusion.155
  173.6 80.6 %all-reduce.8.cloned.1.call-done = f32[768,768]{1,0:T(8,128)} async-done(((f32[768,768]{1,0:T(8,128)}), f32[768,768]{1,0:T(8,128)}) %all-reduce.8.cloned.1.call-update) | async-done | bytes 2359312 | tf_op jit(solution)/shard_map/psum | solution.py:121
  261.1 14.3 %convert_reduce_fusion = (f32[1536]{0:T(1024)}, bf16[768,1536]{1,0:T(8,128)(2,1)S(1)}, f32[768,1536]{1,0:T(8,128)}) fusion(f32[768,1536]{1,0:T(8,128)S(1)} %fusion.82, f32[1536]{0:T(1024)S(1)} %copy-done.53, bf16[768,768]{1,0:T(8,128)(2,1)S(1)} %copy-done.18, bf16[1536,768]{1,0:T(8,128)(2,1)S(1)} %copy-done), kind=kOutput, calls=%fused_computation.56 | convolution fusion | flops 1900411392 | bytes 15347712 | tf_op jit(solution)/shard_map/dot_general | solution.py:38
  280.3 4.9 multiply_convert_fusion.1
  289.6 59.4 %all-reduce.10.cloned.1.call-done = f32[768,768]{1,0:T(8,128)} async-done(((f32[768,768]{1,0:T(8,128)}), f32[768,768]{1,0:T(8,128)}) %all-reduce.10.cloned.1.call-update) | async-done | bytes 2359312 | tf_op jit(solution)/shard_map/psum | solution.py:141
  349.0 4.0 multiply_reduce_fusion.1
  357.3 137.6 %while.29 = (s32[]{:T(128)}, bf16[6,768,64]{1,2,0:T(8,128)(2,1)S(1)}, f32[6,3840,64]{1,2,0:T(8,128)}, f32[6,3840,64]{1,2,0:T(8,128)}, bf16[6,768,64]{2,1,0:T(8,1...) while((s32[]{:T(128)}, ...), condition=%wide.region_15.16_spmd.clone, body=%wide.region_13.15_spmd.clone.sunk | while | flops 1917271296 | bytes 117906592 | solution.py:162
  361.0 5.0 multiply_reduce_fusion.5
  366.0 4.0 multiply_convert_fusion.3
  370.0 5.0 fusion.165
  383.9 5.0 multiply_reduce_fusion.5
  388.9 4.0 multiply_convert_fusion.3
  392.9 5.0 fusion.165
  406.9 5.0 multiply_reduce_fusion.5
  411.8 4.0 multiply_convert_fusion.3
  415.9 5.0 fusion.165
  429.8 5.0 multiply_reduce_fusion.5
  434.7 4.0 multiply_convert_fusion.3
  438.8 5.0 fusion.165
  452.7 5.0 multiply_reduce_fusion.5
  457.7 4.0 multiply_convert_fusion.3
  461.7 5.0 fusion.165
  475.6 5.0 multiply_reduce_fusion.5
  480.6 4.0 multiply_convert_fusion.3
  484.6 5.0 fusion.165
  496.5 5.1 bitcast_convert_fusion
  509.6 6.9 collective-permute-start.15
  518.8 19.1 %collective-permute-done.11 = bf16[768,384]{0,1:T(8,128)(2,1)S(1)} collective-permute-done((bf16[768,384]{0,1:T(8,128)(2,1)S(1)}, bf16[768,384]{0,1:T(8,128)(2,1)S(1)}, u32[]{:S(2)}, u32[]{:S(2)}) %collective-permute-start.11) | collective-permute-done | bytes 589856 | tf_op jit(solution)/shard_map/ppermute | solution.py:13
  543.3 13.5 %collective-permute-done.15 = bf16[768,384]{0,1:T(8,128)(2,1)S(1)} collective-permute-done((bf16[768,384]{0,1:T(8,128)(2,1)S(1)}, bf16[768,384]{0,1:T(8,128)(2,1)S(1)}, u32[]{:S(2)}, u32[]{:S(2)}) %collective-permute-start.15) | collective-permute-done | bytes 589856 | tf_op jit(solution)/shard_map/ppermute | solution.py:13
  558.0 21.4 %collective-permute-done.12 = bf16[768,384]{0,1:T(8,128)(2,1)S(1)} collective-permute-done((bf16[768,384]{0,1:T(8,128)(2,1)S(1)}, bf16[768,384]{0,1:T(8,128)(2,1)S(1)}, u32[]{:S(2)}, u32[]{:S(2)}) %collective-permute-start.12) | collective-permute-done | bytes 589856 | tf_op jit(solution)/shard_map/ppermute | solution.py:13
  582.5 6.4 fusion.99
  588.9 4.5 fusion.81
  605.3 48.7 %all-reduce.14.cloned.1.call-done = (bf16[768,768]{1,0:T(8,128)(2,1)}, bf16[768,768]{1,0:T(8,128)(2,1)}) async-done(((bf16[768,768]{1,0:T(8,128)(2,1)}, bf16[768,768]{1,0:T(8,128)(2,1)}), (bf16[768,768]{1,0:T(8,128)(2,1)}, bf16[768,768]{1,0:T(8,128)(2,1)})) %all-reduce.14.cloned.1.call-update) | async-done | bytes 2359312 | tf_op jit(solution)/shard_map/psum | solution.py:130
  661.7 65.9 %all-reduce = (f32[768]{0:T(1024)}, f32[768]{0:T(1024)}, f32[384]{0:T(512)}, f32[384]{0:T(512)}, f32[768]{0:T(1024)}, /*index=5*/f32[768]{0:T(1024)}, f32[768]{0:T(1024)}, f32[1536]{0:T(1024)}, f32[768]{0:T(1024)}) all-reduce(f32[768]{0:T(1024)} %get-tuple-element.181, ...), channel_id=1, replica_groups=mesh['dp'=16,'tensor'=2] {'dp'}, use_global_device_ids=true, to_apply=%region_20.21 | all-reduce | flops 6912 | bytes 55296 | tf_op jit(solution)/shard_map/psum | solution.py:219
  730.3 191.6 %all-reduce.12.cloned.1.call-done = (f32[768,384]{1,0:T(8,128)}, f32[768,384]{1,0:T(8,128)}, f32[768,384]{1,0:T(8,128)}, f32[384,768]{1,0:T(8,128)}, f32[768,1536]{1,0:T(8,128)}, /*index=5*/f32[1536,768]{1,0:T(8,128)}) async-done(((f32[768,384]{1,0:T(8,128)}, f32[768,384]{1,0:T(8,128)}, f32[768,384]{1,0:T(8,128)}, f32[384,768]{1,0:T(8,128)}, f32[768,1536]{1,0:T(8,128)}, /*index=5*/f32[1536,768]{1,0:T(8,128)}), ...) | async-done | bytes 14155792 | tf_op jit(solution)/shard_map/psum | solution.py:219
  (310 shorter events, 226.3 us)
Async XLA Ops:
  7.2 253.9 %copy-start = (bf16[1536,768]{1,0:T(8,128)(2,1)S(1)}, bf16[1536,768]{1,0:T(8,128)(2,1)}, u32[]{:S(2)}) copy-start(bf16[1536,768]{1,0:T(8,128)(2,1)} %param.37) | copy-start | bytes 7077892
  7.2 247.1 %all-reduce.8.cloned.1.call-start = ((), (), s32[]{:S(2)}) async-start(), calls=%async_computation | async-start | bytes 4718592 | tf_op jit(solution)/shard_map/psum | solution.py:121
  12.8 12.9 %copy-start.59 = (bf16[384]{0:T(512)(128)(2,1)S(1)}, bf16[384]{0:T(512)(128)(2,1)}, u32[]{:S(2)}) copy-start(bf16[384]{0:T(512)(128)(2,1)} %param.30) | copy-start | bytes 2308
  12.8 12.9 %copy-start.28 = (bf16[768,384]{1,0:T(8,128)(2,1)S(1)}, bf16[768,384]{1,0:T(8,128)(2,1)}, u32[]{:S(2)}) copy-start(bf16[768,384]{1,0:T(8,128)(2,1)} %param.29) | copy-start | bytes 1769476
  13.4 20.0 %copy-start.10 = (bf16[768,768]{1,0:T(8,128)(2,1)}, bf16[768,768]{1,0:T(8,128)(2,1)S(1)}, u32[]{:S(2)}) copy-start(bf16[768,768]{1,0:T(8,128)(2,1)S(1)} %fusion.63) | copy-start | bytes 3538948
  15.0 18.4 %copy-start.60 = (bf16[384]{0:T(512)(128)(2,1)S(1)}, bf16[384]{0:T(512)(128)(2,1)}, u32[]{:S(2)}) copy-start(bf16[384]{0:T(512)(128)(2,1)} %param.27) | copy-start | bytes 2308
  15.0 18.4 %copy-start.31 = (bf16[768,384]{1,0:T(8,128)(2,1)S(1)}, bf16[768,384]{1,0:T(8,128)(2,1)}, u32[]{:S(2)}) copy-start(bf16[768,384]{1,0:T(8,128)(2,1)} %param.26) | copy-start | bytes 1769476
  15.0 38.0 %collective-permute-start = (bf16[768,384]{1,0:T(8,128)(2,1)}, bf16[768,384]{1,0:T(8,128)(2,1)}, u32[]{:S(2)}, u32[]{:S(2)}) collective-permute-start(bf16[768,384]{1,0:T(8,128)(2,1)} %convolution_convert_fusion.2), channel_id=1, source_target_pairs={{0,4},{2,6},{4,8},{6,10},{8,12},{10,14},{12,16},{14,18},{16,20},{1... | collective-permute-start | bytes 1769480 | tf_op jit(solution)/shard_map/ppermute | solution.py:13
  20.8 36.2 %collective-permute-start.1 = (bf16[768,384]{1,0:T(8,128)(2,1)}, bf16[768,384]{1,0:T(8,128)(2,1)}, u32[]{:S(2)}, u32[]{:S(2)}) collective-permute-start(bf16[768,384]{1,0:T(8,128)(2,1)} %convolution_convert_fusion.2), channel_id=1, source_target_pairs={{0,2},{2,4},{4,6},{6,8},{8,10},{10,12},{12,14},{14,16},{16,18},{18... | collective-permute-start | bytes 1769480 | tf_op jit(solution)/shard_map/ppermute | solution.py:13
  23.1 39.1 %collective-permute-start.2 = (bf16[768,384]{1,0:T(8,128)(2,1)}, bf16[768,384]{1,0:T(8,128)(2,1)}, u32[]{:S(2)}, u32[]{:S(2)}) collective-permute-start(bf16[768,384]{1,0:T(8,128)(2,1)} %convolution_convert_fusion.2), channel_id=1, source_target_pairs={{2,0},{4,2},{6,4},{8,6},{10,8},{12,10},{14,12},{16,14},{18,16},{20... | collective-permute-start | bytes 1769480 | tf_op jit(solution)/shard_map/ppermute | solution.py:13
  24.4 41.5 %collective-permute-start.3 = (bf16[768,384]{1,0:T(8,128)(2,1)}, bf16[768,384]{1,0:T(8,128)(2,1)}, u32[]{:S(2)}, u32[]{:S(2)}) collective-permute-start(bf16[768,384]{1,0:T(8,128)(2,1)} %convolution_convert_fusion.2), channel_id=1, source_target_pairs={{4,0},{6,2},{8,4},{10,6},{12,8},{14,10},{16,12},{18,14},{20,16},{2... | collective-permute-start | bytes 1769480 | tf_op jit(solution)/shard_map/ppermute | solution.py:13
  27.3 51.5 %collective-permute-start.4 = (bf16[768,384]{1,0:T(8,128)(2,1)}, bf16[768,384]{1,0:T(8,128)(2,1)}, u32[]{:S(2)}, u32[]{:S(2)}) collective-permute-start(bf16[768,384]{1,0:T(8,128)(2,1)} %fusion.70), channel_id=1, source_target_pairs={{0,4},{2,6},{4,8},{6,10},{8,12},{10,14},{12,16},{14,18},{16,20},{1... | collective-permute-start | bytes 1769480 | tf_op jit(solution)/shard_map/ppermute | solution.py:13
  53.0 27.8 %collective-permute-start.5 = (bf16[768,384]{1,0:T(8,128)(2,1)}, bf16[768,384]{1,0:T(8,128)(2,1)}, u32[]{:S(2)}, u32[]{:S(2)}) collective-permute-start(bf16[768,384]{1,0:T(8,128)(2,1)} %fusion.70), channel_id=1, source_target_pairs={{0,2},{2,4},{4,6},{6,8},{8,10},{10,12},{12,14},{14,16},{16,18},{18... | collective-permute-start | bytes 1769480 | tf_op jit(solution)/shard_map/ppermute | solution.py:13
  57.0 27.6 %collective-permute-start.6 = (bf16[768,384]{1,0:T(8,128)(2,1)}, bf16[768,384]{1,0:T(8,128)(2,1)}, u32[]{:S(2)}, u32[]{:S(2)}) collective-permute-start(bf16[768,384]{1,0:T(8,128)(2,1)} %fusion.70), channel_id=1, source_target_pairs={{2,0},{4,2},{6,4},{8,6},{10,8},{12,10},{14,12},{16,14},{18,16},{20... | collective-permute-start | bytes 1769480 | tf_op jit(solution)/shard_map/ppermute | solution.py:13
  62.2 26.3 %collective-permute-start.7 = (bf16[768,384]{1,0:T(8,128)(2,1)}, bf16[768,384]{1,0:T(8,128)(2,1)}, u32[]{:S(2)}, u32[]{:S(2)}) collective-permute-start(bf16[768,384]{1,0:T(8,128)(2,1)} %fusion.70), channel_id=1, source_target_pairs={{4,0},{6,2},{8,4},{10,6},{12,8},{14,10},{16,12},{18,14},{20,16},{2... | collective-permute-start | bytes 1769480 | tf_op jit(solution)/shard_map/ppermute | solution.py:13
  167.3 5.7 copy-start.55
  170.8 178.2 %all-reduce.10.cloned.1.call-start = ((), (), s32[]{:S(2)}) async-start(), calls=%async_computation.1 | async-start | bytes 4718592 | tf_op jit(solution)/shard_map/psum | solution.py:141
  173.0 180.0 %copy-start.45 = (f32[768]{0:T(1024)}, f32[768]{0:T(1024)S(1)}, u32[]{:S(2)}) copy-start(f32[768]{0:T(1024)S(1)} %convert_element_type.175) | copy-start | bytes 9220
  256.4 96.6 %copy-start.41 = (f32[768]{0:T(1024)}, f32[768]{0:T(1024)S(1)}, u32[]{:S(2)}) copy-start(f32[768]{0:T(1024)S(1)} %broadcast_multiply_fusion) | copy-start | bytes 9220
  258.9 94.1 %copy-start.47 = (f32[768]{0:T(1024)}, f32[768]{0:T(1024)S(1)}, u32[]{:S(2)}) copy-start(f32[768]{0:T(1024)S(1)} %fusion.80) | copy-start | bytes 9220
  261.1 14.3 %copy-start.21 = (f32[768,1536]{1,0:T(8,128)}, f32[768,1536]{1,0:T(8,128)S(1)}, u32[]{:S(2)}) copy-start(f32[768,1536]{1,0:T(8,128)S(1)} %fusion.82) | copy-start | bytes 14155780
  280.2 373.7 %all-reduce.14.cloned.1.call-start = ((), (), s32[]{:S(2)}) async-start(), calls=%async_computation.3 | async-start | bytes 4718592 | tf_op jit(solution)/shard_map/psum | solution.py:130
  289.6 63.4 %copy-start.4 = (f32[768,768]{1,0:T(8,128)S(1)}, f32[768,768]{1,0:T(8,128)}, u32[]{:S(2)}) copy-start(f32[768,768]{1,0:T(8,128)} %copy-done.3) | copy-start | bytes 7077892
  494.9 98.6 %copy-start.14 = (bf16[6,768,64]{1,2,0:T(8,128)(2,1)}, bf16[6,768,64]{1,2,0:T(8,128)(2,1)S(1)}, u32[]{:S(2)}) copy-start(bf16[6,768,64]{1,2,0:T(8,128)(2,1)S(1)} %get-tuple-element.111) | copy-start | bytes 1769476
  501.8 36.1 %collective-permute-start.11 = (bf16[768,384]{0,1:T(8,128)(2,1)S(1)}, bf16[768,384]{0,1:T(8,128)(2,1)S(1)}, u32[]{:S(2)}, u32[]{:S(2)}) collective-permute-start(bf16[768,384]{0,1:T(8,128)(2,1)S(1)} %bitcast.188), channel_id=1, source_target_pairs={{0,4},{2,6},{4,8},{6,10},{8,12},{10,14},{12,16},{14,18},{16,20},{1... | collective-permute-start | bytes 1769480 | tf_op jit(solution)/shard_map/ppermute | solution.py:13
  505.2 34.0 %collective-permute-start.10 = (bf16[768,384]{0,1:T(8,128)(2,1)S(1)}, bf16[768,384]{0,1:T(8,128)(2,1)S(1)}, u32[]{:S(2)}, u32[]{:S(2)}) collective-permute-start(bf16[768,384]{0,1:T(8,128)(2,1)S(1)} %bitcast.187), channel_id=1, source_target_pairs={{0,2},{2,4},{4,6},{6,8},{8,10},{10,12},{12,14},{14,16},{16,18},{18... | collective-permute-start | bytes 1769480 | tf_op jit(solution)/shard_map/ppermute | solution.py:13
  506.7 33.8 %collective-permute-start.9 = (bf16[768,384]{0,1:T(8,128)(2,1)S(1)}, bf16[768,384]{0,1:T(8,128)(2,1)S(1)}, u32[]{:S(2)}, u32[]{:S(2)}) collective-permute-start(bf16[768,384]{0,1:T(8,128)(2,1)S(1)} %bitcast.185), channel_id=1, source_target_pairs={{2,0},{4,2},{6,4},{8,6},{10,8},{12,10},{14,12},{16,14},{18,16},{20... | collective-permute-start | bytes 1769480 | tf_op jit(solution)/shard_map/ppermute | solution.py:13
  508.0 34.0 %collective-permute-start.8 = (bf16[768,384]{0,1:T(8,128)(2,1)S(1)}, bf16[768,384]{0,1:T(8,128)(2,1)S(1)}, u32[]{:S(2)}, u32[]{:S(2)}) collective-permute-start(bf16[768,384]{0,1:T(8,128)(2,1)S(1)} %bitcast.181), channel_id=1, source_target_pairs={{4,0},{6,2},{8,4},{10,6},{12,8},{14,10},{16,12},{18,14},{20,16},{2... | collective-permute-start | bytes 1769480 | tf_op jit(solution)/shard_map/ppermute | solution.py:13
  509.6 8.3 copy-start.32
  509.6 47.2 %collective-permute-start.15 = (bf16[768,384]{0,1:T(8,128)(2,1)S(1)}, bf16[768,384]{0,1:T(8,128)(2,1)S(1)}, u32[]{:S(2)}, u32[]{:S(2)}) collective-permute-start(bf16[768,384]{0,1:T(8,128)(2,1)S(1)} %bitcast.186), channel_id=1, source_target_pairs={{0,4},{2,6},{4,8},{6,10},{8,12},{10,14},{12,16},{14,18},{16,20},{1... | collective-permute-start | bytes 1769480 | tf_op jit(solution)/shard_map/ppermute | solution.py:13
  518.8 23.7 %copy-start.34 = (bf16[768,384]{1,0:T(8,128)(2,1)S(1)}, bf16[768,384]{1,0:T(8,128)(2,1)}, u32[]{:S(2)}) copy-start(bf16[768,384]{1,0:T(8,128)(2,1)} %param.28) | copy-start | bytes 1769476
  537.9 19.0 %collective-permute-start.14 = (bf16[768,384]{0,1:T(8,128)(2,1)S(1)}, bf16[768,384]{0,1:T(8,128)(2,1)S(1)}, u32[]{:S(2)}, u32[]{:S(2)}) collective-permute-start(bf16[768,384]{0,1:T(8,128)(2,1)S(1)} %bitcast.184), channel_id=1, source_target_pairs={{0,2},{2,4},{4,6},{6,8},{8,10},{10,12},{12,14},{14,16},{16,18},{18... | collective-permute-start | bytes 1769480 | tf_op jit(solution)/shard_map/ppermute | solution.py:13
  539.2 18.8 %collective-permute-start.13 = (bf16[768,384]{0,1:T(8,128)(2,1)S(1)}, bf16[768,384]{0,1:T(8,128)(2,1)S(1)}, u32[]{:S(2)}, u32[]{:S(2)}) collective-permute-start(bf16[768,384]{0,1:T(8,128)(2,1)S(1)} %bitcast.183), channel_id=1, source_target_pairs={{2,0},{4,2},{6,4},{8,6},{10,8},{12,10},{14,12},{16,14},{18,16},{20... | collective-permute-start | bytes 1769480 | tf_op jit(solution)/shard_map/ppermute | solution.py:13
  540.5 38.9 %collective-permute-start.12 = (bf16[768,384]{0,1:T(8,128)(2,1)S(1)}, bf16[768,384]{0,1:T(8,128)(2,1)S(1)}, u32[]{:S(2)}, u32[]{:S(2)}) collective-permute-start(bf16[768,384]{0,1:T(8,128)(2,1)S(1)} %bitcast.182), channel_id=1, source_target_pairs={{4,0},{6,2},{8,4},{10,6},{12,8},{14,10},{16,12},{18,14},{20,16},{2... | collective-permute-start | bytes 1769480 | tf_op jit(solution)/shard_map/ppermute | solution.py:13
  542.5 15.6 %copy-start.16 = (bf16[768,384]{0,1:T(8,128)(2,1)}, bf16[768,384]{0,1:T(8,128)(2,1)S(1)}, u32[]{:S(2)}) copy-start(bf16[768,384]{0,1:T(8,128)(2,1)S(1)} %fusion.78) | copy-start | bytes 1769476
  543.3 37.2 %copy-start.29 = (bf16[768,384]{1,0:T(8,128)(2,1)S(1)}, bf16[768,384]{1,0:T(8,128)(2,1)}, u32[]{:S(2)}) copy-start(bf16[768,384]{1,0:T(8,128)(2,1)} %param.29) | copy-start | bytes 1769476
  582.4 6.5 copy-start.5
  582.4 6.5 copy-start.42
  582.4 6.5 copy-start.46
  582.5 6.5 copy-start.48
  582.5 6.5 copy-start.57
  582.5 339.4 %all-reduce.12.cloned.1.call-start = ((), (), s32[]{:S(2)}) async-start(), calls=%async_computation.2 | async-start | bytes 28311552 | tf_op jit(solution)/shard_map/psum | solution.py:219
  582.5 6.4 copy-start.63
  600.7 53.2 %copy-start.7 = (bf16[768,768]{1,0:T(8,128)(2,1)S(1)}, bf16[768,768]{1,0:T(8,128)(2,1)}, u32[]{:S(2)}) copy-start(bf16[768,768]{1,0:T(8,128)(2,1)} %param.22) | copy-start | bytes 3538948
  600.7 53.2 %copy-start.36 = (f32[768]{0:T(1024)S(1)}, f32[768]{0:T(1024)}, u32[]{:S(2)}) copy-start(f32[768]{0:T(1024)} %copy-done.35) | copy-start | bytes 9220
  600.7 53.2 %copy-start.38 = (f32[768]{0:T(1024)S(1)}, f32[768]{0:T(1024)}, u32[]{:S(2)}) copy-start(f32[768]{0:T(1024)} %copy-done.37) | copy-start | bytes 9220
  600.7 56.1 %copy-start.50 = (f32[768]{0:T(1024)S(1)}, f32[768]{0:T(1024)}, u32[]{:S(2)}) copy-start(f32[768]{0:T(1024)} %copy-done.49) | copy-start | bytes 9220
  600.8 56.1 %copy-start.40 = (f32[768]{0:T(1024)S(1)}, f32[768]{0:T(1024)}, u32[]{:S(2)}) copy-start(f32[768]{0:T(1024)} %copy-done.39) | copy-start | bytes 9220
  (43 other events, 140.9 us)
Sparse Core Ops, SparseCore 0:
  171.0 83.2 all-reduce.7
  280.3 68.6 all-reduce.9
  582.5 71.3 all-reduce.13
  660.9 260.8 all-reduce.11
where the time goes:
time: 949 us; the launch traced here: 941 us
  waiting for transfers between devices  446 us (47%)
  matrix products  208 us (22%)
  other arithmetic  82.8 us (9%)
  local copies, waits for them, and re-layouts  81.3 us (9%)
  blocking collectives  65.9 us (7%)
  starting transfers between devices  40.8 us (4%)
  between operations  15 us (2%)
    psum x1, waiting for transfers between devices, on_device(): lax.psum((w_query_grad, query_bias_grad, w_key_grad, w_value_grad, value_...  192 us
    dot_general x24, matrix products, contract_cols(): lax.dot_general(left, right, (((1,), (1,)), ((), ())), preferred_element_...  88.8 us
    psum x1, waiting for transfers between devices, on_device(): lax.psum(matmul(attn_mixed, w_out), 'tensor') + out_bias.astype(jnp.float32)  80.6 us
    dot_general x18, matrix products, matmul(): return jnp.dot(left, right, preferred_element_type=jnp.float32)  69.8 us
    ppermute x16, waiting for transfers between devices, from_behind(): return lax.ppermute(block, axis, route)  66 us
    psum x1, blocking collectives, on_device(): lax.psum((w_query_grad, query_bias_grad, w_key_grad, w_value_grad, value_...  65.9 us
    psum x1, waiting for transfers between devices, on_device(): mlp_in_grad = lax.psum(contract_cols(pre_grad, w_fc1), 'tensor')  59.4 us
    dot_general x18, matrix products, contract_rows(): lax.dot_general(left, right, (((0,), (0,)), ((), ())), preferred_element_...  49.8 us
  transfers between devices with their start and end apart: 20, of which 10 were waited for; matrix products, arithmetic and copies ran while one was open for 9% of the time, Pallas kernels for 0%

commit v1 on v0

--- a/solution.py
+++ b/solution.py
@@ -5,6 +5,12 @@
 
 HEAD_DIM = 64
 REACH = 2
+
+
+def summed_here(x, mesh_axis):
+    blocks = lax.all_gather(x, mesh_axis, axis=0, tiled=False)
+    total = blocks.sum(axis=0)
+    return total
 
 
 def from_behind(block, axis, distance):
@@ -127,7 +133,7 @@
     preact = matmul(mlp_input, w_fc1) + fc1_bias.astype(jnp.float32)
     activated_full, gelu_back = jax.vjp(exact_gelu, preact)
     activated = activated_full.astype(jnp.bfloat16)
-    mlp_total = lax.psum(matmul(activated, w_fc2).astype(jnp.bfloat16), "tensor").astype(
+    mlp_total = summed_here(matmul(activated, w_fc2).astype(jnp.bfloat16), "tensor").astype(
         jnp.float32
     ) + fc2_bias.astype(jnp.float32)
     layer_out = (residual + mlp_total).astype(jnp.bfloat16)

time: 949 us -> 998 us (1.052)
  matrix products: 208 us -> 229 us
  local copies, waits for them, and re-layouts: 81.3 us -> 95.9 us
  waiting for transfers between devices: 446 us -> 456 us
    all_gather x0 -> x1, waiting for transfers between devices: none -> 34.5 us  [summed_here(): blocks = lax.all_gather(x, mesh_axis, axis=0, tiled=False)]
    while x12 -> x24, local copies, waits for them, and re-layouts: 0.02 us -> 15.5 us
    dot_general x18, matrix products: 49.8 us -> 62.4 us  [contract_rows(): lax.dot_general(left, right, (((0,), (0,)), ((), ())), preferred_element_...]
    psum x1, waiting for transfers between devices: 48.7 us -> 36.1 us  [on_device(): lax.psum(attn_in_part.astype(jnp.bfloat16), 'tensor').astype(jnp.float32)]
    psum x1, waiting for transfers between devices: 59.4 us -> 47.4 us  [on_device(): mlp_in_grad = lax.psum(contract_cols(pre_grad, w_fc1), 'tensor')]
    unnamed x146 -> x124, local copies, waits for them, and re-layouts: 46.8 us -> 46.9 us
  transfers between devices with their start and end apart: 20 -> 21, of which waited for: 10 -> 9; matrix products, arithmetic and copies ran while one was open for 9% -> 9% of each run, Pallas kernels for 0% -> 0%
where the time goes in v1:
time: 998 us; the launch traced here: 990 us
  waiting for transfers between devices  456 us (46%)
  matrix products  229 us (23%)
  local copies, waits for them, and re-layouts  95.9 us (10%)
  other arithmetic  84.9 us (9%)
  blocking collectives  65.9 us (7%)
  starting transfers between devices  43 us (4%)
  between operations  15 us (2%)
    psum x1, waiting for transfers between devices, on_device(): lax.psum((w_query_grad, query_bias_grad, w_key_grad, w_value_grad, value_...  192 us
    dot_general x24, matrix products, contract_cols(): lax.dot_general(left, right, (((1,), (1,)), ((), ())), preferred_element_...  88.8 us
    psum x1, waiting for transfers between devices, on_device(): lax.psum(matmul(attn_mixed, w_out), 'tensor') + out_bias.astype(jnp.float32)  80.7 us
    dot_general x18, matrix products, matmul(): return jnp.dot(left, right, preferred_element_type=jnp.float32)  77.6 us
    psum x1, blocking collectives, on_device(): lax.psum((w_query_grad, query_bias_grad, w_key_grad, w_value_grad, value_...  65.9 us
    ppermute x16, waiting for transfers between devices, from_behind(): return lax.ppermute(block, axis, route)  65.3 us
    dot_general x18, matrix products, contract_rows(): lax.dot_general(left, right, (((0,), (0,)), ((), ())), preferred_element_...  62.4 us
    psum x1, waiting for transfers between devices, on_device(): mlp_in_grad = lax.psum(contract_cols(pre_grad, w_fc1), 'tensor')  47.4 us
  transfers between devices with their start and end apart: 21, of which 9 were waited for; matrix products, arithmetic and copies ran while one was open for 9% of the time, Pallas kernels for 0%

profile of v1, /device:TPU:0, one launch (start us, length us, event | category | flops | bytes accessed | tf_op | source)
XLA Modules:
  0.0 990.1 jit_solution(4125132774011656002)
XLA Ops:
  13.6 5.7 collective-permute-start.4
  25.7 6.1 collective-permute-start
  42.5 8.9 collective-permute-done.4
  66.3 4.5 copy.41
  70.8 6.5 copy.43
  88.9 4.5 copy.40
  93.4 6.5 copy.42
  100.7 99.6 %while.28 = (s32[]{:T(128)}, bf16[6,768,64]{1,2,0:T(8,128)(2,1)}, f32[6,768]{1,0:T(8,128)}, bf16[6,768,64]{2,1,0:T(8,128)(2,1)}, bf16[6,3840,64]{2,1,0:T(8,128)(...) while((s32[]{:T(128)}, bf16[6,768,64]{1,2,0:T(8,128)(2,1)}, ...), condition=%wide.region_5.6_spmd.clone, body=%wide.region_2.5_spmd.clone.sunk | while | flops 781565184 | bytes 84894856 | solution.py:125
  109.8 7.6 fusion.155
  126.3 7.6 fusion.155
  142.9 7.6 fusion.155
  159.5 7.6 fusion.155
  176.1 7.6 fusion.155
  192.7 7.6 fusion.155
  206.6 80.7 %all-reduce.7.cloned.1.call-done = f32[768,768]{1,0:T(8,128)} async-done(((f32[768,768]{1,0:T(8,128)}), f32[768,768]{1,0:T(8,128)}) %all-reduce.7.cloned.1.call-update) | async-done | bytes 2359312 | tf_op jit(solution)/shard_map/psum | solution.py:127
  294.2 14.3 %convert_reduce_fusion = (f32[1536]{0:T(1024)}, bf16[768,1536]{1,0:T(8,128)(2,1)S(1)}, f32[768,1536]{1,0:T(8,128)}) fusion(f32[768,1536]{1,0:T(8,128)S(1)} %fusion.82, f32[1536]{0:T(1024)S(1)} %copy-done.42, bf16[768,768]{1,0:T(8,128)(2,1)S(1)} %copy-done.15, bf16[1536,768]{1,0:T(8,128)(2,1)S(1)} %copy-done), kind=kOutput, calls=%fused_computation.56 | convolution fusion | flops 1900411392 | bytes 15347712 | tf_op jit(solution)/shard_map/dot_general | solution.py:44
  313.4 4.9 multiply_convert_fusion.1
  324.2 6.0 fusion.99
  330.2 4.5 fusion.81
  334.8 47.4 %all-reduce.9.cloned.1.call-done = f32[768,768]{1,0:T(8,128)} async-done(((f32[768,768]{1,0:T(8,128)}), f32[768,768]{1,0:T(8,128)}) %all-reduce.9.cloned.1.call-update) | async-done | bytes 2359312 | tf_op jit(solution)/shard_map/psum | solution.py:147
  385.9 34.5 %all-gather.3.cloned.1.call-done = bf16[1536,768]{1,0:T(8,128)(2,1)} async-done(((bf16[768,768]{1,0:T(8,128)(2,1)}), bf16[1536,768]{1,0:T(8,128)(2,1)}) %all-gather.3.cloned.1.call-update) | async-done | bytes 2359312 | tf_op jit(solution)/shard_map/all_gather | solution.py:11
  430.8 137.7 %while.29 = (s32[]{:T(128)}, bf16[6,768,64]{1,2,0:T(8,128)(2,1)S(1)}, f32[6,3840,64]{1,2,0:T(8,128)}, f32[6,3840,64]{1,2,0:T(8,128)}, bf16[6,768,64]{2,1,0:T(8,1...) while((s32[]{:T(128)}, ...), condition=%wide.region_15.16_spmd.clone, body=%wide.region_13.15_spmd.clone.sunk | while | flops 1917271296 | bytes 117906576 | solution.py:168
  434.5 5.0 multiply_reduce_fusion.5
  439.5 4.0 multiply_convert_fusion.3
  443.4 5.0 fusion.166
  457.4 5.0 multiply_reduce_fusion.5
  462.4 4.0 multiply_convert_fusion.3
  466.4 5.0 fusion.166
  480.4 5.0 multiply_reduce_fusion.5
  485.3 4.0 multiply_convert_fusion.3
  489.3 5.0 fusion.166
  503.4 5.0 multiply_reduce_fusion.5
  508.3 4.0 multiply_convert_fusion.3
  512.3 5.0 fusion.166
  526.3 5.0 multiply_reduce_fusion.5
  531.2 4.0 multiply_convert_fusion.3
  535.2 5.0 fusion.166
  549.2 5.0 multiply_reduce_fusion.5
  554.1 4.0 multiply_convert_fusion.3
  558.1 5.0 fusion.166
  568.5 5.1 bitcast_convert_fusion
  588.7 42.1 %collective-permute-done.11 = bf16[768,384]{0,1:T(8,128)(2,1)S(1)} collective-permute-done((bf16[768,384]{0,1:T(8,128)(2,1)S(1)}, bf16[768,384]{0,1:T(8,128)(2,1)S(1)}, u32[]{:S(2)}, u32[]{:S(2)}) %collective-permute-start.11) | collective-permute-done | bytes 589856 | tf_op jit(solution)/shard_map/ppermute | solution.py:19
  630.8 5.8 collective-permute-start.14
  636.6 4.1 collective-permute-start.15
  642.0 12.5 %collective-permute-done.15 = bf16[768,384]{0,1:T(8,128)(2,1)S(1)} collective-permute-done((bf16[768,384]{0,1:T(8,128)(2,1)S(1)}, bf16[768,384]{0,1:T(8,128)(2,1)S(1)}, u32[]{:S(2)}, u32[]{:S(2)}) %collective-permute-start.15) | collective-permute-done | bytes 589856 | tf_op jit(solution)/shard_map/ppermute | solution.py:19
  667.1 36.1 %all-reduce.11.cloned.1.call-done = bf16[768,768]{1,0:T(8,128)(2,1)} async-done(((bf16[768,768]{1,0:T(8,128)(2,1)}), bf16[768,768]{1,0:T(8,128)(2,1)}) %all-reduce.11.cloned.1.call-update) | async-done | bytes 1179664 | tf_op jit(solution)/shard_map/psum | solution.py:206
  712.9 65.9 %all-reduce = (f32[768]{0:T(1024)}, f32[768]{0:T(1024)}, f32[384]{0:T(512)}, f32[384]{0:T(512)}, f32[768]{0:T(1024)}, /*index=5*/f32[768]{0:T(1024)}, f32[768]{0:T(1024)}, f32[1536]{0:T(1024)}, f32[768]{0:T(1024)}) all-reduce(f32[768]{0:T(1024)} %get-tuple-element.181, ...), channel_id=1, replica_groups=mesh['dp'=16,'tensor'=2] {'dp'}, use_global_device_ids=true, to_apply=%region_20.21 | all-reduce | flops 6912 | bytes 55296 | tf_op jit(solution)/shard_map/psum | solution.py:225
  778.9 192.2 %all-reduce.13.cloned.1.call-done = (f32[768,384]{1,0:T(8,128)}, f32[768,384]{1,0:T(8,128)}, f32[768,384]{1,0:T(8,128)}, f32[384,768]{1,0:T(8,128)}, f32[768,1536]{1,0:T(8,128)}, /*index=5*/f32[1536,768]{1,0:T(8,128)}) async-done(((f32[768,384]{1,0:T(8,128)}, f32[768,384]{1,0:T(8,128)}, f32[768,384]{1,0:T(8,128)}, f32[384,768]{1,0:T(8,128)}, f32[768,1536]{1,0:T(8,128)}, /*index=5*/f32[1536,768]{1,0:T(8,128)}), ...) | async-done | bytes 14155792 | tf_op jit(solution)/shard_map/psum | solution.py:225
  (303 shorter events, 246.9 us)
Async XLA Ops:
  7.2 286.9 %copy-start = (bf16[1536,768]{1,0:T(8,128)(2,1)S(1)}, bf16[1536,768]{1,0:T(8,128)(2,1)}, u32[]{:S(2)}) copy-start(bf16[1536,768]{1,0:T(8,128)(2,1)} %param.37) | copy-start | bytes 7077892
  7.2 280.1 %all-reduce.7.cloned.1.call-start = ((), (), s32[]{:S(2)}) async-start(), calls=%async_computation | async-start | bytes 4718592 | tf_op jit(solution)/shard_map/psum | solution.py:127
  11.4 12.7 %copy-start.29 = (bf16[768,384]{1,0:T(8,128)(2,1)S(1)}, bf16[768,384]{1,0:T(8,128)(2,1)}, u32[]{:S(2)}) copy-start(bf16[768,384]{1,0:T(8,128)(2,1)} %param.28) | copy-start | bytes 1769476
  11.9 19.9 %copy-start.10 = (bf16[768,768]{1,0:T(8,128)(2,1)}, bf16[768,768]{1,0:T(8,128)(2,1)S(1)}, u32[]{:S(2)}) copy-start(bf16[768,768]{1,0:T(8,128)(2,1)S(1)} %fusion.63) | copy-start | bytes 3538948
  12.0 19.9 %copy-start.50 = (bf16[384]{0:T(512)(128)(2,1)S(1)}, bf16[384]{0:T(512)(128)(2,1)}, u32[]{:S(2)}) copy-start(bf16[384]{0:T(512)(128)(2,1)} %param.27) | copy-start | bytes 2308
  12.0 19.9 %copy-start.27 = (bf16[768,384]{1,0:T(8,128)(2,1)S(1)}, bf16[768,384]{1,0:T(8,128)(2,1)}, u32[]{:S(2)}) copy-start(bf16[768,384]{1,0:T(8,128)(2,1)} %param.26) | copy-start | bytes 1769476
  13.6 37.8 %collective-permute-start.4 = (bf16[768,384]{1,0:T(8,128)(2,1)}, bf16[768,384]{1,0:T(8,128)(2,1)}, u32[]{:S(2)}, u32[]{:S(2)}) collective-permute-start(bf16[768,384]{1,0:T(8,128)(2,1)} %fusion.70), channel_id=1, source_target_pairs={{0,4},{2,6},{4,8},{6,10},{8,12},{10,14},{12,16},{14,18},{16,20},{1... | collective-permute-start | bytes 1769480 | tf_op jit(solution)/shard_map/ppermute | solution.py:19
  19.3 36.2 %collective-permute-start.5 = (bf16[768,384]{1,0:T(8,128)(2,1)}, bf16[768,384]{1,0:T(8,128)(2,1)}, u32[]{:S(2)}, u32[]{:S(2)}) collective-permute-start(bf16[768,384]{1,0:T(8,128)(2,1)} %fusion.70), channel_id=1, source_target_pairs={{0,2},{2,4},{4,6},{6,8},{8,10},{10,12},{12,14},{14,16},{16,18},{18... | collective-permute-start | bytes 1769480 | tf_op jit(solution)/shard_map/ppermute | solution.py:19
  21.5 39.1 %collective-permute-start.6 = (bf16[768,384]{1,0:T(8,128)(2,1)}, bf16[768,384]{1,0:T(8,128)(2,1)}, u32[]{:S(2)}, u32[]{:S(2)}) collective-permute-start(bf16[768,384]{1,0:T(8,128)(2,1)} %fusion.70), channel_id=1, source_target_pairs={{2,0},{4,2},{6,4},{8,6},{10,8},{12,10},{14,12},{16,14},{18,16},{20... | collective-permute-start | bytes 1769480 | tf_op jit(solution)/shard_map/ppermute | solution.py:19
  22.8 41.6 %collective-permute-start.7 = (bf16[768,384]{1,0:T(8,128)(2,1)}, bf16[768,384]{1,0:T(8,128)(2,1)}, u32[]{:S(2)}, u32[]{:S(2)}) collective-permute-start(bf16[768,384]{1,0:T(8,128)(2,1)} %fusion.70), channel_id=1, source_target_pairs={{4,0},{6,2},{8,4},{10,6},{12,8},{14,10},{16,12},{18,14},{20,16},{2... | collective-permute-start | bytes 1769480 | tf_op jit(solution)/shard_map/ppermute | solution.py:19
  25.7 51.6 %collective-permute-start = (bf16[768,384]{1,0:T(8,128)(2,1)}, bf16[768,384]{1,0:T(8,128)(2,1)}, u32[]{:S(2)}, u32[]{:S(2)}) collective-permute-start(bf16[768,384]{1,0:T(8,128)(2,1)} %convolution_convert_fusion.2), channel_id=1, source_target_pairs={{0,4},{2,6},{4,8},{6,10},{8,12},{10,14},{12,16},{14,18},{16,20},{1... | collective-permute-start | bytes 1769480 | tf_op jit(solution)/shard_map/ppermute | solution.py:19
  51.4 27.9 %collective-permute-start.1 = (bf16[768,384]{1,0:T(8,128)(2,1)}, bf16[768,384]{1,0:T(8,128)(2,1)}, u32[]{:S(2)}, u32[]{:S(2)}) collective-permute-start(bf16[768,384]{1,0:T(8,128)(2,1)} %convolution_convert_fusion.2), channel_id=1, source_target_pairs={{0,2},{2,4},{4,6},{6,8},{8,10},{10,12},{12,14},{14,16},{16,18},{18... | collective-permute-start | bytes 1769480 | tf_op jit(solution)/shard_map/ppermute | solution.py:19
  55.5 27.7 %collective-permute-start.2 = (bf16[768,384]{1,0:T(8,128)(2,1)}, bf16[768,384]{1,0:T(8,128)(2,1)}, u32[]{:S(2)}, u32[]{:S(2)}) collective-permute-start(bf16[768,384]{1,0:T(8,128)(2,1)} %convolution_convert_fusion.2), channel_id=1, source_target_pairs={{2,0},{4,2},{6,4},{8,6},{10,8},{12,10},{14,12},{16,14},{18,16},{20... | collective-permute-start | bytes 1769480 | tf_op jit(solution)/shard_map/ppermute | solution.py:19
  60.6 26.3 %collective-permute-start.3 = (bf16[768,384]{1,0:T(8,128)(2,1)}, bf16[768,384]{1,0:T(8,128)(2,1)}, u32[]{:S(2)}, u32[]{:S(2)}) collective-permute-start(bf16[768,384]{1,0:T(8,128)(2,1)} %convolution_convert_fusion.2), channel_id=1, source_target_pairs={{4,0},{6,2},{8,4},{10,6},{12,8},{14,10},{16,12},{18,14},{20,16},{2... | collective-permute-start | bytes 1769480 | tf_op jit(solution)/shard_map/ppermute | solution.py:19
  200.3 5.7 copy-start.43
  203.8 178.3 %all-reduce.9.cloned.1.call-start = ((), (), s32[]{:S(2)}) async-start(), calls=%async_computation.1 | async-start | bytes 4718592 | tf_op jit(solution)/shard_map/psum | solution.py:147
  289.4 4.7 copy-start.6
  294.1 14.3 %copy-start.18 = (f32[768,1536]{1,0:T(8,128)}, f32[768,1536]{1,0:T(8,128)S(1)}, u32[]{:S(2)}) copy-start(f32[768,1536]{1,0:T(8,128)S(1)} %fusion.82) | copy-start | bytes 14155780
  313.4 107.0 %all-gather.3.cloned.1.call-start = ((), (), s32[]{:S(2)}) async-start(), calls=%async_computation.3 | async-start | bytes 3538944 | tf_op jit(solution)/shard_map/all_gather | solution.py:11
  322.8 380.4 %all-reduce.11.cloned.1.call-start = ((), (), s32[]{:S(2)}) async-start(), calls=%async_computation.2 | async-start | bytes 2359296 | tf_op jit(solution)/shard_map/psum | solution.py:206
  324.1 6.0 copy-start.7
  324.1 6.0 copy-start.45
  324.2 6.0 copy-start.53
  443.4 5.0 copy-start.2
  466.4 5.0 copy-start.2
  489.3 5.0 copy-start.2
  512.3 5.0 copy-start.2
  535.2 5.0 copy-start.2
  558.1 5.0 copy-start.2
  573.8 13.4 %collective-permute-start.10 = (bf16[768,384]{0,1:T(8,128)(2,1)S(1)}, bf16[768,384]{0,1:T(8,128)(2,1)S(1)}, u32[]{:S(2)}, u32[]{:S(2)}) collective-permute-start(bf16[768,384]{0,1:T(8,128)(2,1)S(1)} %bitcast.190), channel_id=1, source_target_pairs={{0,2},{2,4},{4,6},{6,8},{8,10},{10,12},{12,14},{14,16},{16,18},{18... | collective-permute-start | bytes 1769480 | tf_op jit(solution)/shard_map/ppermute | solution.py:19
  575.6 55.2 %collective-permute-start.11 = (bf16[768,384]{0,1:T(8,128)(2,1)S(1)}, bf16[768,384]{0,1:T(8,128)(2,1)S(1)}, u32[]{:S(2)}, u32[]{:S(2)}) collective-permute-start(bf16[768,384]{0,1:T(8,128)(2,1)S(1)} %bitcast.189), channel_id=1, source_target_pairs={{0,4},{2,6},{4,8},{6,10},{8,12},{10,14},{12,16},{14,18},{16,20},{1... | collective-permute-start | bytes 1769480 | tf_op jit(solution)/shard_map/ppermute | solution.py:19
  579.2 57.5 %collective-permute-start.8 = (bf16[768,384]{0,1:T(8,128)(2,1)S(1)}, bf16[768,384]{0,1:T(8,128)(2,1)S(1)}, u32[]{:S(2)}, u32[]{:S(2)}) collective-permute-start(bf16[768,384]{0,1:T(8,128)(2,1)S(1)} %bitcast.187), channel_id=1, source_target_pairs={{4,0},{6,2},{8,4},{10,6},{12,8},{14,10},{16,12},{18,14},{20,16},{2... | collective-permute-start | bytes 1769480 | tf_op jit(solution)/shard_map/ppermute | solution.py:19
  580.5 60.3 %collective-permute-start.9 = (bf16[768,384]{0,1:T(8,128)(2,1)S(1)}, bf16[768,384]{0,1:T(8,128)(2,1)S(1)}, u32[]{:S(2)}, u32[]{:S(2)}) collective-permute-start(bf16[768,384]{0,1:T(8,128)(2,1)S(1)} %bitcast.183), channel_id=1, source_target_pairs={{2,0},{4,2},{6,4},{8,6},{10,8},{12,10},{14,12},{16,14},{18,16},{20... | collective-permute-start | bytes 1769480 | tf_op jit(solution)/shard_map/ppermute | solution.py:19
  582.1 59.9 %collective-permute-start.12 = (bf16[768,384]{0,1:T(8,128)(2,1)S(1)}, bf16[768,384]{0,1:T(8,128)(2,1)S(1)}, u32[]{:S(2)}, u32[]{:S(2)}) collective-permute-start(bf16[768,384]{0,1:T(8,128)(2,1)S(1)} %bitcast.188), channel_id=1, source_target_pairs={{4,0},{6,2},{8,4},{10,6},{12,8},{14,10},{16,12},{18,14},{20,16},{2... | collective-permute-start | bytes 1769480 | tf_op jit(solution)/shard_map/ppermute | solution.py:19
  587.2 53.9 %copy-start.30 = (bf16[768,384]{1,0:T(8,128)(2,1)S(1)}, bf16[768,384]{1,0:T(8,128)(2,1)}, u32[]{:S(2)}) copy-start(bf16[768,384]{1,0:T(8,128)(2,1)} %param.28) | copy-start | bytes 1769476
  587.3 54.7 %collective-permute-start.13 = (bf16[768,384]{0,1:T(8,128)(2,1)S(1)}, bf16[768,384]{0,1:T(8,128)(2,1)S(1)}, u32[]{:S(2)}, u32[]{:S(2)}) collective-permute-start(bf16[768,384]{0,1:T(8,128)(2,1)S(1)} %bitcast.186), channel_id=1, source_target_pairs={{2,0},{4,2},{6,4},{8,6},{10,8},{12,10},{14,12},{16,14},{18,16},{20... | collective-permute-start | bytes 1769480 | tf_op jit(solution)/shard_map/ppermute | solution.py:19
  630.8 11.2 %collective-permute-start.14 = (bf16[768,384]{0,1:T(8,128)(2,1)S(1)}, bf16[768,384]{0,1:T(8,128)(2,1)S(1)}, u32[]{:S(2)}, u32[]{:S(2)}) collective-permute-start(bf16[768,384]{0,1:T(8,128)(2,1)S(1)} %bitcast.185), channel_id=1, source_target_pairs={{0,2},{2,4},{4,6},{6,8},{8,10},{10,12},{12,14},{14,16},{16,18},{18... | collective-permute-start | bytes 1769480 | tf_op jit(solution)/shard_map/ppermute | solution.py:19
  636.6 17.8 %collective-permute-start.15 = (bf16[768,384]{0,1:T(8,128)(2,1)S(1)}, bf16[768,384]{0,1:T(8,128)(2,1)S(1)}, u32[]{:S(2)}, u32[]{:S(2)}) collective-permute-start(bf16[768,384]{0,1:T(8,128)(2,1)S(1)} %bitcast.184), channel_id=1, source_target_pairs={{0,4},{2,6},{4,8},{6,10},{8,12},{10,14},{12,16},{14,18},{16,20},{1... | collective-permute-start | bytes 1769480 | tf_op jit(solution)/shard_map/ppermute | solution.py:19
  642.0 13.6 %copy-start.25 = (bf16[768,384]{1,0:T(8,128)(2,1)S(1)}, bf16[768,384]{1,0:T(8,128)(2,1)}, u32[]{:S(2)}) copy-start(bf16[768,384]{1,0:T(8,128)(2,1)} %param.29) | copy-start | bytes 1769476
  657.5 313.6 %all-reduce.13.cloned.1.call-start = ((), (), s32[]{:S(2)}) async-start(), calls=%async_computation.4 | async-start | bytes 28311552 | tf_op jit(solution)/shard_map/psum | solution.py:225
  666.2 37.0 %copy-start.5 = (bf16[768,768]{1,0:T(8,128)(2,1)S(1)}, bf16[768,768]{1,0:T(8,128)(2,1)}, u32[]{:S(2)}) copy-start(bf16[768,768]{1,0:T(8,128)(2,1)} %param.22) | copy-start | bytes 3538948
  666.2 37.0 %copy-start.32 = (f32[768]{0:T(1024)S(1)}, f32[768]{0:T(1024)}, u32[]{:S(2)}) copy-start(f32[768]{0:T(1024)} %copy-done.31) | copy-start | bytes 9220
  666.2 37.0 %copy-start.34 = (f32[768]{0:T(1024)S(1)}, f32[768]{0:T(1024)}, u32[]{:S(2)}) copy-start(f32[768]{0:T(1024)} %copy-done.33) | copy-start | bytes 9220
  666.3 40.5 %copy-start.36 = (f32[768]{0:T(1024)S(1)}, f32[768]{0:T(1024)}, u32[]{:S(2)}) copy-start(f32[768]{0:T(1024)} %copy-done.35) | copy-start | bytes 9220
  667.1 42.9 %copy-start.16 = (bf16[768,768]{1,0:T(8,128)(2,1)S(1)}, bf16[768,768]{1,0:T(8,128)(2,1)}, u32[]{:S(2)}) copy-start(bf16[768,768]{1,0:T(8,128)(2,1)} %param.39) | copy-start | bytes 3538948
  667.1 42.9 %copy-start.38 = (f32[768]{0:T(1024)S(1)}, f32[768]{0:T(1024)}, u32[]{:S(2)}) copy-start(f32[768]{0:T(1024)} %copy-done.37) | copy-start | bytes 9220
  703.2 6.8 copy-start.9
  703.2 6.8 copy-start.12
  (39 other events, 115.1 us)
Sparse Core Ops, SparseCore 0:
  203.9 83.3 all-reduce.6
  313.5 68.6 all-reduce.8
  384.3 36.0 all-gather.2
  657.6 45.5 all-reduce.10
  710.2 260.9 all-reduce.12
